TPU v7x, 128 devices: a whole 4x4x4 slice. The times are simulated.
128 devices in a mesh: ctx: 32 (over z, x, core), tp: 4 (over y).
Axes of the slice: x: 4, y: 4, z: 4, core: 2. Of those that a mesh axis runs over, the one named last changes fastest.
Arguments:
- hidden_states: bfloat16 [3072, 8192], P('ctx', 'tp'), may hold values from -6 to 6
- counts: int32 [32], P('ctx'), may hold values from 24 to 72, as said below
- selected: int32 [32, 72], P('ctx'), may hold values from 0 to 95, as said below
- router_weight: float32 [3072], P('ctx'), may hold values from 0.25 to 1.5
- norm_gain: float32 [8192], P('tp'), may hold values from 0.25 to 1.75
- w_gate: bfloat16 [8192, 28672], P('tp', 'ctx'), may hold values from -0.0625 to 0.0625
- w_up: bfloat16 [8192, 28672], P('tp', 'ctx'), may hold values from -0.0625 to 0.0625
- w_down: bfloat16 [28672, 8192], P('ctx', 'tp'), may hold values from -0.03125 to 0.03125
Outputs:
- block_out: bfloat16 [3072, 8192], P('ctx', 'tp')
Inputs may be any that keep to these rules, and one draw needn't show every extreme that they name: The counts sum to 1536; for every shard s the counts of the shards before s sum to between s * 48 - 48 // 4 and s * 48 + 48 // 4. `selected`: the entries of a row are distinct; only the first counts[s] entries of row s are used.
All inputs are finite; a program needn't handle non-finite values.
Results may differ from a plain program's by a relative error of at most 0.014.
Values may be sent and summed in bfloat16 or wider, within the bound.
A program may use at most 128 MiB of HBM per device.

v0:
```python
import jax
import jax.numpy as jnp
from jax import lax
from jax.sharding import PartitionSpec as P

D = 8192


def body(hidden_states, counts, selected, router_weight, norm_gain, w_gate, w_up, w_down):
    chosen = selected[0]
    how_many = counts[0]
    most_rows = chosen.shape[0]
    tok_local = hidden_states.shape[0]
    active = jnp.arange(most_rows, dtype=jnp.int32) < how_many
    picked_f = hidden_states[chosen].astype(jnp.float32)
    squares = jnp.sum(picked_f * picked_f, axis=-1)
    totals = lax.psum(squares, "tp")
    mean_sq = totals / D
    scaled = picked_f * lax.rsqrt(mean_sq + 1e-05)[:, None] * norm_gain[None, :]
    normed = jnp.where(active[:, None], scaled, 0.0).astype(jnp.bfloat16)
    piece = lax.all_gather(normed, "ctx", axis=0, tiled=True)
    gate_part = jnp.dot(piece, w_gate, preferred_element_type=jnp.float32)
    up_part = jnp.dot(piece, w_up, preferred_element_type=jnp.float32)
    partial_units = jnp.stack([gate_part, up_part], axis=1)
    shares = lax.psum_scatter(
        partial_units.astype(jnp.bfloat16), "tp", scatter_dimension=2, tiled=True
    ).astype(jnp.float32)
    hidden_share = (jax.nn.silu(shares[:, 0]) * shares[:, 1]).astype(jnp.bfloat16)
    hidden = lax.all_gather(hidden_share, "tp", axis=1, tiled=True)
    ffn_block = lax.psum_scatter(
        jnp.dot(hidden, w_down, preferred_element_type=jnp.float32).astype(jnp.bfloat16),
        "ctx",
        scatter_dimension=0,
        tiled=True,
    )
    scale_rows = router_weight[chosen] * active.astype(jnp.float32)
    delta = ffn_block.astype(jnp.float32) * scale_rows[:, None]
    onehot = (jnp.arange(tok_local, dtype=jnp.int32)[:, None] == chosen[None, :]).astype(
        jnp.float32
    )
    added = jnp.dot(
        onehot, delta, precision=lax.Precision.HIGHEST, preferred_element_type=jnp.float32
    )
    return (hidden_states.astype(jnp.float32) + added).astype(jnp.bfloat16)


def solution(mesh):
    placed = (
        P("ctx", "tp"),
        P("ctx"),
        P("ctx", None),
        P("ctx"),
        P("tp"),
        P("tp", "ctx"),
        P("tp", "ctx"),
        P("ctx", "tp"),
    )
    return jax.shard_map(
        body, mesh=mesh, in_specs=placed, out_specs=P("ctx", "tp"), check_vma=False
    )
```

profile of v0, /device:TPU:0, one launch (start us, length us, event | category | flops | bytes accessed | tf_op | source)
XLA Modules:
  0.0 466.2 jit_solution(7711977555393432972)
XLA Ops:
  7.2 0.7 fusion.12
  7.9 2.1 gather_fusion
  10.0 0.2 fusion.4
  10.1 10.8 %psum.7 = f32[72]{0:T(128)S(1)} all-reduce(f32[72]{0:T(128)S(1)} %fusion.4), channel_id=1, replica_groups=mesh['ctx'=32,'tp'=4] {'tp'}, use_global_device_ids=true, to_apply=%region_1.0 | all-reduce | flops 72 | bytes 576 | tf_op jit(solution)/shard_map/psum | solution.py:17
  21.0 1.6 fusion.7
  22.6 0.0 all-reduce.3.cloned.1.call-start
  22.6 55.7 %all-gather.3.cloned.1.call-done = bf16[2304,2048]{1,0:T(8,128)(2,1)} async-done(((bf16[72,2048]{1,0:T(8,128)(2,1)}), bf16[2304,2048]{1,0:T(8,128)(2,1)}) %all-gather.3.cloned.1.call-update) | async-done | bytes 9437200 | tf_op jit(solution)/shard_map/all_gather | solution.py:21
  78.3 13.7 %fusion.1 = bf16[2304,1,896]{2,0,1:T(8,128)(2,1)S(1)} fusion(bf16[2304,2048]{1,0:T(8,128)(2,1)} %all-gather.3.cloned.1.call-done, bf16[2048,896]{1,0:T(8,128)(2,1)} %param.14), kind=kOutput, calls=%fused_computation.7 | convolution fusion | flops 8457781248 | bytes 17235968 | tf_op jit(solution)/shard_map/dot_general | solution.py:23
  92.1 11.3 %fusion = bf16[2304,1,896]{2,0,1:T(8,128)(2,1)} fusion(bf16[2304,2048]{1,0:T(8,128)(2,1)S(1)} %copy-done.3, bf16[2048,896]{1,0:T(8,128)(2,1)S(1)} %copy-done.4), kind=kOutput, calls=%fused_computation.6 | convolution fusion | flops 8457781248 | bytes 17235968 | tf_op jit(solution)/shard_map/dot_general | solution.py:22
  103.4 6.2 %pad_maximum_fusion = bf16[2304,2,896]{2,0,1:T(8,128)(2,1)} fusion(bf16[2304,1,896]{2,0,1:T(8,128)(2,1)S(1)} %fusion.1, bf16[2304,1,896]{2,0,1:T(8,128)(2,1)} %fusion), kind=kLoop, calls=%fused_computation.3 | loop fusion | flops 4128768 | bytes 16515072 | tf_op jit(solution)/shard_map/stack | solution.py:24
  109.6 23.2 %copy.9 = bf16[2304,2,896]{0,1,2:T(2,128)(2,1)} copy(bf16[2304,2,896]{2,0,1:T(8,128)(2,1)} %pad_maximum_fusion) | data formatting | bytes 16515072 | tf_op jit(solution)/shard_map/stack | solution.py:24
  132.8 0.2 all-gather.5.cloned.1.call-start
  133.1 0.4 copy-done.5
  133.4 0.6 dynamic-slice
  134.7 155.9 %all-reduce.3.cloned.1.call-done = bf16[2304,2,896]{0,1,2:T(2,128)(2,1)} async-done(((bf16[2304,2,896]{0,1,2:T(2,128)(2,1)}), bf16[2304,2,896]{0,1,2:T(2,128)(2,1)}) %all-reduce.3.cloned.1.call-update) | async-done | bytes 8257552
  290.5 3.0 dynamic-slice_convert_fusion
  293.5 3.2 fusion.13
  296.7 1.6 fusion.3
  298.3 0.0 reduce-scatter.2.cloned.1.call-start
  298.4 47.7 %all-gather.5.cloned.1.call-done = bf16[2304,896]{0,1:T(8,128)(2,1)} async-done(((bf16[2304,224]{0,1:T(8,128)(2,1)}), bf16[2304,896]{0,1:T(8,128)(2,1)}) %all-gather.5.cloned.1.call-update) | async-done | bytes 4128784 | tf_op jit(solution)/shard_map/all_gather | solution.py:29
  346.0 15.3 %convolution_convert_fusion = bf16[2304,2048]{1,0:T(8,128)(2,1)} fusion(bf16[2304,896]{0,1:T(8,128)(2,1)} %all-gather.5.cloned.1.call-done, bf16[896,2048]{1,0:T(8,128)(2,1)} %param.15), kind=kOutput, calls=%fused_computation.2 | convolution fusion | flops 8460435456 | bytes 17235968 | tf_op jit(solution)/shard_map/dot_general | solution.py:31
  361.3 1.2 gather_fusion.1
  362.6 94.7 %reduce-scatter.2.cloned.1.call-done = bf16[72,2048]{1,0:T(8,128)(2,1)} async-done(((bf16[2304,2048]{1,0:T(8,128)(2,1)}), bf16[72,2048]{1,0:T(8,128)(2,1)}) %reduce-scatter.2.cloned.1.call-update) | async-done | bytes 294928 | tf_op jit(solution)/shard_map/reduce_scatter | solution.py:30
  457.3 2.4 fusion.2
  (20 shorter events, 0.1 us)
Async XLA Ops:
  6.5 354.8 %copy-start = (f32[96]{0:T(128)S(1)}, f32[96]{0:T(128)}, u32[]{:S(2)}) copy-start(f32[96]{0:T(128)} %param.11) | copy-start | bytes 1156
  6.5 71.7 %all-gather.3.cloned.1.call-start = ((), (), s32[]{:S(2)}) async-start(), calls=%async_computation.1 | async-start | bytes 9732096 | tf_op jit(solution)/shard_map/all_gather | solution.py:21
  22.6 268.0 %all-reduce.3.cloned.1.call-start = ((), (), s32[]{:S(2)}) async-start(), calls=%async_computation.4 | async-start | bytes 16515072
  78.3 13.8 %copy-start.3 = (bf16[2304,2048]{1,0:T(8,128)(2,1)S(1)}, bf16[2304,2048]{1,0:T(8,128)(2,1)}, u32[]{:S(2)}) copy-start(bf16[2304,2048]{1,0:T(8,128)(2,1)} %all-gather.3.cloned.1.call-done) | copy-start | bytes 28311556
  78.3 13.8 %copy-start.4 = (bf16[2048,896]{1,0:T(8,128)(2,1)S(1)}, bf16[2048,896]{1,0:T(8,128)(2,1)}, u32[]{:S(2)}) copy-start(bf16[2048,896]{1,0:T(8,128)(2,1)} %param.13) | copy-start | bytes 11010052
  132.8 0.7 copy-start.5
  132.8 213.2 %all-gather.5.cloned.1.call-start = ((), (), s32[]{:S(2)}) async-start(), calls=%async_computation.2 | async-start | bytes 5160960 | tf_op jit(solution)/shard_map/all_gather | solution.py:29
  298.3 159.0 %reduce-scatter.2.cloned.1.call-start = ((), (), s32[]{:S(2)}) async-start(), calls=%async_computation.3 | async-start | bytes 9732096 | tf_op jit(solution)/shard_map/reduce_scatter | solution.py:30
  361.3 96.0 %copy-start.1 = (bf16[96,2048]{1,0:T(8,128)(2,1)S(1)}, bf16[96,2048]{1,0:T(8,128)(2,1)}, u32[]{:S(2)}) copy-start(bf16[96,2048]{1,0:T(8,128)(2,1)} %param.8) | copy-start | bytes 1179652
  361.3 96.0 %copy-start.2 = (s32[1,72]{1,0:T(1,128)S(1)}, s32[1,72]{1,0:T(1,128)}, u32[]{:S(2)}) copy-start(s32[1,72]{1,0:T(1,128)} %param.10) | copy-start | bytes 868
Sparse Core Ops, SparseCore 0:
  22.7 55.5 all-gather.2
  132.9 157.5 all-reduce.2
  298.4 47.5 all-gather.4
  361.4 95.8 reduce-scatter.1
where the time goes:
time: 467 us; the launch traced here: 466 us
  waiting for transfers between devices  354 us (76%)
  matrix products  42.7 us (9%)
  local copies, waits for them, and re-layouts  30.7 us (7%)
  between operations  14.5 us (3%)
  other arithmetic  13.1 us (3%)
  blocking collectives  10.8 us (2%)
    unnamed x5, waiting for transfers between devices  156 us
    reduce_scatter x1, waiting for transfers between devices, body(): lax.psum_scatter(jnp.dot(hidden, w_down, preferred_element_type=jnp.float...  94.7 us
    all_gather x1, waiting for transfers between devices, body(): piece = lax.all_gather(normed, 'ctx', axis=0, tiled=True)  55.7 us
    all_gather x1, waiting for transfers between devices, body(): hidden = lax.all_gather(hidden_share, 'tp', axis=1, tiled=True)  47.7 us
    another operation x1, local copies, waits for them, and re-layouts, body(): partial_units = jnp.stack([gate_part, up_part], axis=1)  23.2 us
    dot_general x1, matrix products, body(): jnp.dot(hidden, w_down, preferred_element_type=jnp.float32)  15.3 us
    dot_general x1, matrix products, body(): up_part = jnp.dot(piece, w_up, preferred_element_type=jnp.float32)  13.7 us
    dot_general x1, matrix products, body(): gate_part = jnp.dot(piece, w_gate, preferred_element_type=jnp.float32)  11.3 us
  transfers between devices with their start and end apart: 4, of which 4 were waited for; matrix products, arithmetic and copies ran while one was open for 0% of the time, Pallas kernels for 0%

commit v1 on v0

v1 whole, which is shorter than its diff:
```python
import jax
import jax.numpy as jnp
from jax import lax
from jax.experimental import pallas as pl
from jax.experimental.pallas import tpu as pltpu
from jax.sharding import PartitionSpec as P

MESH = pl.DeviceIdType.MESH
F32 = jnp.float32
BF16 = jnp.bfloat16
N_SEM = 128


def body(hidden, counts, selected, router_weight, norm_gain, w_gate, w_up, w_down, n_ctx, n_tp):
    tok, feat = hidden.shape
    most = selected.shape[1]
    units = w_gate.shape[1]
    width = feat * n_tp
    rows = most * 2 // 3
    edge = 16
    nx, nz, ny = 4, n_ctx // 8, n_tp
    half = feat // 2
    own = ny and (nx * 2 * rows) // ny

    def kernel(counts_ref, sel_ref, rw_ref, gain_ref, hid_ref, wg_hbm, wu_hbm, wd_hbm, out_ref,
               w_gu, w_dn, sq, cnt, ztot, to_prev, to_next, from_next, from_prev,
               x_buf, part, r1, r2, h_buf, y_buf, sib_buf, q1, q2, t_buf, zr,
               tail_next, tail_prev, edge_next, edge_prev, load_sem, send_sem, recv_sem):
        ctx = lax.axis_index("ctx")
        y = lax.axis_index("tp")
        z, q = ctx // 8, ctx % 8
        x, c = q // 2, q % 2

        def at(zz, xx, cc):
            return (zz * nx + xx) * 2 + cc

        xp, xm, x2 = (x + 1) % nx, (x + nx - 1) % nx, (x + 2) % nx
        zp, zm = (z + 1) % nz, (z + nz - 1) % nz
        yp, ym, y2 = (y + 1) % ny, (y + ny - 1) % ny, (y + 2) % ny
        sib = (at(z, x, 1 - c), y)
        d_xp, d_xm = (at(z, xp, c), y), (at(z, xm, c), y)
        d_zp, d_zm = (at(zp, x, c), y), (at(zm, x, c), y)
        d_yp, d_ym = (ctx, yp), (ctx, ym)
        d_next, d_prev = ((ctx + 1) % n_ctx, y), ((ctx + n_ctx - 1) % n_ctx, y)

        loads = []
        for i, (src, dst) in enumerate((
            (wg_hbm, w_gu.at[:, pl.ds(0, units)]),
            (wu_hbm, w_gu.at[:, pl.ds(units, units)]),
            (wd_hbm, w_dn),
        )):
            load = pltpu.make_async_copy(src, dst, load_sem.at[i])
            load.start()
            loads.append(load)

        used = []

        def copy(src, dst, dev):
            i = len(used)
            d = pltpu.make_async_remote_copy(
                src_ref=src, dst_ref=dst, send_sem=send_sem.at[i], recv_sem=recv_sem.at[i],
                device_id=dev, device_id_type=MESH)
            used.append(d)
            d.start()
            return d

        row_peers = [(at(z, (q + j) % 8 // 2, (q + j) % 8 % 2), y) for j in range(1, 8)]
        z_peers = [(at((z + j) % nz, x, c), y) for j in range(1, nz)]
        y_peers = [(ctx, (y + j) % ny) for j in range(1, ny)]

        barrier = pltpu.get_barrier_semaphore()
        peers = row_peers + z_peers + y_peers + [d_next, d_prev]
        for dev in peers:
            pl.semaphore_signal(barrier, inc=1, device_id=dev, device_id_type=MESH)

        n_f = counts_ref[0].astype(F32)
        cnt[q] = jnp.full((8, 128), n_f, F32)
        hid = hid_ref[...].astype(F32)
        sq[y] = jnp.broadcast_to(jnp.sum(hid * hid, axis=-1, keepdims=True), (tok, 128))

        pl.semaphore_wait(barrier, len(peers))

        c_row = [copy(cnt.at[q], cnt.at[q], dev) for dev in row_peers]
        c_sq = [copy(sq.at[y], sq.at[y], dev) for dev in y_peers]
        for d in c_row:
            d.wait_recv()
        before = jnp.zeros((8, 128), F32)
        total = jnp.zeros((8, 128), F32)
        for j in range(8):
            before = before + cnt[j] * jnp.where(j < q, 1.0, 0.0).astype(F32)
            total = total + cnt[j]
        ztot[z] = total
        c_z = [copy(ztot.at[z], ztot.at[z], dev) for dev in z_peers]

        for d in c_sq:
            d.wait_recv()
        sums = sq[0]
        for j in range(1, ny):
            sums = sums + sq[j]
        scale = lax.rsqrt(sums[:, 0:1] / width + 1e-05)
        normed = (hid_ref[...].astype(F32) * scale * gain_ref[...]).astype(BF16)

        for d in c_z:
            d.wait_recv()
        for j in range(nz):
            before = before + ztot[j] * jnp.where(j < z, 1.0, 0.0).astype(F32)
        excess = (before - (ctx * rows).astype(F32))[0:1, 0:1]
        ids = lax.broadcasted_iota(jnp.int32, (tok, most), 0)
        rank = lax.broadcasted_iota(jnp.int32, (tok, most), 1).astype(F32)
        match = jnp.where((sel_ref[...] == ids) & (rank < n_f), 1.0, 0.0).astype(F32).astype(BF16)

        def chosen(count, offset):
            slot = lax.broadcasted_iota(jnp.int32, (count, most), 0).astype(F32) + offset
            place = lax.broadcasted_iota(jnp.int32, (count, most), 1).astype(F32) + excess
            shift = jnp.where(slot == place, 1.0, 0.0).astype(F32).astype(BF16)
            return lax.dot_general(
                shift, match, (((1,), (1,)), ((), ())), preferred_element_type=F32).astype(BF16)

        to_prev[...] = jnp.dot(chosen(edge, -edge), normed, preferred_element_type=F32).astype(BF16)
        c_prev = copy(to_prev, from_next, d_prev)
        to_next[...] = jnp.dot(chosen(edge, rows), normed, preferred_element_type=F32).astype(BF16)
        c_next = copy(to_next, from_prev, d_next)
        mine = jnp.dot(chosen(rows, 0), normed, preferred_element_type=F32)
        x_buf[0, x, c] = mine.astype(BF16)
        c_next.wait_recv()
        x_buf[0, x, c, pl.ds(0, edge)] = (
            x_buf[0, x, c, pl.ds(0, edge)].astype(F32) + from_prev[...].astype(F32)).astype(BF16)
        c_prev.wait_recv()
        x_buf[0, x, c, pl.ds(rows - edge, edge)] = (
            x_buf[0, x, c, pl.ds(rows - edge, edge)].astype(F32) + from_next[...].astype(F32)
        ).astype(BF16)

        lo, hi = pl.ds(0, half), pl.ds(half, half)
        rel = [x, xm, xp, x2]
        g_sib = [[None] * 4 for _ in range(4)]
        g_up, g_dn = [None] * 4, [None] * 4

        def spread(i):
            xb = rel[i]
            g_up[i] = copy(x_buf.at[0, xb, c], x_buf.at[3, xb, c], d_zp)
            g_dn[i] = copy(x_buf.at[0, xb, c], x_buf.at[1, xb, c], d_zm)
            share(0, i)

        def share(k, i):
            xb = rel[i]
            g_sib[k][i] = copy(x_buf.at[k, xb, c], x_buf.at[k, xb, c], sib)

        a_p = copy(x_buf.at[0, x, c], x_buf.at[0, x, c], d_xp)
        a_m = copy(x_buf.at[0, x, c], x_buf.at[0, x, c], d_xm)
        spread(0)
        a_p.wait_recv()
        b_p = copy(x_buf.at[0, xm, c, :, lo], x_buf.at[0, xm, c, :, lo], d_xp)
        a_m.wait_recv()
        b_m = copy(x_buf.at[0, xp, c, :, hi], x_buf.at[0, xp, c, :, hi], d_xm)
        spread(1)
        spread(2)
        b_p.wait_recv()
        b_m.wait_recv()
        spread(3)

        loads[0].wait()
        loads[1].wait()

        steps = (2 * units) // 256
        y_first, y_second, y_gather, y_pass = {}, {}, {}, {}

        def gate_up(k):
            for i in range(4):
                g_sib[k][i].wait_recv()

            def tile(j, carry):
                cols = pl.ds(pl.multiple_of(j * 256, 256), 256)
                res = jnp.dot(x_buf[k].reshape(nx * 2 * rows, feat), w_gu[:, cols],
                              preferred_element_type=F32)
                part[k, :, :, cols] = res.astype(BF16).reshape(ny, own, 256)
                return carry

            lax.fori_loop(0, steps, tile, 0)
            gate, up = pl.ds(0, units), pl.ds(units, units)
            y_first[k] = (copy(part.at[k, y2, :, gate], r1.at[k, 0], d_yp),
                          copy(part.at[k, y2, :, up], r1.at[k, 1], d_ym))
            y_second[k] = [copy(part.at[k, yp, :, up], r2.at[k, 0, 1], d_yp),
                           copy(part.at[k, ym, :, gate], r2.at[k, 1, 0], d_ym)]

        def combine(k):
            gate, up = pl.ds(0, units), pl.ds(units, units)
            y_first[k][0].wait_recv()
            part[k, yp, :, gate] = (
                part[k, yp, :, gate].astype(F32) + r1[k, 0].astype(F32)).astype(BF16)
            y_second[k].append(copy(part.at[k, yp, :, gate], r2.at[k, 0, 0], d_yp))
            y_first[k][1].wait_recv()
            part[k, ym, :, up] = (
                part[k, ym, :, up].astype(F32) + r1[k, 1].astype(F32)).astype(BF16)
            y_second[k].append(copy(part.at[k, ym, :, up], r2.at[k, 1, 1], d_ym))

        def activate(k):
            gate, up = pl.ds(0, units), pl.ds(units, units)
            for d in y_second[k]:
                d.wait_recv()
            g = part[k, y, :, gate].astype(F32) + r2[k, 0, 0].astype(F32) + r2[k, 1, 0].astype(F32)
            u = part[k, y, :, up].astype(F32) + r2[k, 0, 1].astype(F32) + r2[k, 1, 1].astype(F32)
            h_buf[k, y] = (g / (1.0 + jnp.exp(-g)) * u).astype(BF16)
            y_gather[k] = (copy(h_buf.at[k, y], h_buf.at[k, y], d_yp),
                           copy(h_buf.at[k, y], h_buf.at[k, y], d_ym))

        def pass_on(k):
            first, second = pl.ds(0, own // 2), pl.ds(own // 2, own // 2)
            y_gather[k][0].wait_recv()
            f_p = copy(h_buf.at[k, ym, first], h_buf.at[k, ym, first], d_yp)
            y_gather[k][1].wait_recv()
            f_m = copy(h_buf.at[k, yp, second], h_buf.at[k, yp, second], d_ym)
            y_pass[k] = (f_p, f_m)

        s_core, s_first, s_second, s_z = {}, {}, {}, {}

        def down(k):
            for d in y_pass[k]:
                d.wait_recv()

            def tile(j, carry):
                cols = pl.ds(pl.multiple_of(j * 256, 256), 256)
                res = jnp.dot(h_buf[k].reshape(nx * 2 * rows, units), w_dn[:, cols],
                              preferred_element_type=F32)
                y_buf[k, :, :, :, cols] = res.astype(BF16).reshape(nx, 2, rows, 256)
                return carry

            lax.fori_loop(0, feat // 256, tile, 0)
            s_core[k] = copy(y_buf.at[k, :, 1 - c], sib_buf.at[k], sib)

        def fold(k):
            s_core[k].wait_recv()
            for i in (3, 1, 2, 0):
                xb = rel[i]
                y_buf[k, xb, c] = (
                    y_buf[k, xb, c].astype(F32) + sib_buf[k, xb].astype(F32)).astype(BF16)
                if i == 3:
                    s_first[k] = (copy(y_buf.at[k, x2, c, :, lo], q1.at[k, 0], d_xp),
                                  copy(y_buf.at[k, x2, c, :, hi], q1.at[k, 1], d_xm))
                    s_second[k] = []
                if i == 1:
                    s_second[k].append(copy(y_buf.at[k, xm, c, :, lo], q2.at[k, 1, 0], d_xm))
                if i == 2:
                    s_second[k].append(copy(y_buf.at[k, xp, c, :, hi], q2.at[k, 0, 1], d_xp))

        def fold_on(k):
            s_first[k][0].wait_recv()
            y_buf[k, xp, c, :, lo] = (
                y_buf[k, xp, c, :, lo].astype(F32) + q1[k, 0].astype(F32)).astype(BF16)
            s_second[k].append(copy(y_buf.at[k, xp, c, :, lo], q2.at[k, 0, 0], d_xp))
            s_first[k][1].wait_recv()
            y_buf[k, xm, c, :, hi] = (
                y_buf[k, xm, c, :, hi].astype(F32) + q1[k, 1].astype(F32)).astype(BF16)
            s_second[k].append(copy(y_buf.at[k, xm, c, :, hi], q2.at[k, 1, 1], d_xm))

        def settle(k):
            for d in s_second[k]:
                d.wait_recv()
            for i, cols in enumerate((lo, hi)):
                t_buf[k, :, cols] = (
                    y_buf[k, x, c, :, cols].astype(F32) + q2[k, 0, i].astype(F32)
                    + q2[k, 1, i].astype(F32)).astype(BF16)
            if k:
                s_z[k] = copy(t_buf.at[k], zr.at[(nz - k) % nz - 1], z_peers[k - 1])

        gate_up(0)
        forward = []
        for i in range(4):
            xb = rel[i]
            g_up[i].wait_recv()
            share(3, i)
            if i in (0, 2):
                forward.append(copy(x_buf.at[3, xb, c], x_buf.at[2, xb, c], d_zp))
            g_dn[i].wait_recv()
            share(1, i)
            if i in (1, 3):
                forward.append(copy(x_buf.at[1, xb, c], x_buf.at[2, xb, c], d_zm))
        combine(0)
        gate_up(1)
        activate(0)
        for i in range(4):
            forward[i].wait_recv()
            share(2, i)
        combine(1)
        gate_up(2)
        pass_on(0)
        loads[2].wait()
        down(0)
        activate(1)
        fold(0)
        combine(2)
        gate_up(3)
        pass_on(1)
        down(1)
        fold_on(0)
        activate(2)
        settle(0)
        fold(1)
        combine(3)
        pass_on(2)
        down(2)
        fold_on(1)
        activate(3)
        settle(1)
        fold(2)
        pass_on(3)
        fold_on(2)
        down(3)
        settle(2)
        fold(3)
        fold_on(3)
        settle(3)

        ffn = t_buf[0].astype(F32)
        for k in range(1, nz):
            s_z[k].wait_recv()
        for k in range(1, nz):
            ffn = ffn + zr[k - 1].astype(F32)
        t_buf[0] = ffn.astype(BF16)
        tail_prev[...] = t_buf[0, pl.ds(0, edge)]
        e_prev = copy(tail_prev, edge_next, d_prev)
        tail_next[...] = t_buf[0, pl.ds(rows - edge, edge)]
        e_next = copy(tail_next, edge_prev, d_next)

        span = rows + 2 * edge
        slot = lax.broadcasted_iota(jnp.int32, (most, span), 1).astype(F32) - edge
        place = lax.broadcasted_iota(jnp.int32, (most, span), 0).astype(F32) + excess
        shift = jnp.where(slot == place, 1.0, 0.0).astype(F32).astype(BF16)
        pick = jnp.dot(match, shift, preferred_element_type=F32).astype(BF16)
        line = lax.broadcasted_iota(jnp.int32, (tok, tok), 0)
        col = lax.broadcasted_iota(jnp.int32, (tok, tok), 1)
        weight = jnp.sum(jnp.where(line == col, rw_ref[...], 0.0), axis=-1, keepdims=True)
        e_prev.wait_recv()
        e_next.wait_recv()
        rows_all = jnp.concatenate([edge_prev[...], t_buf[0], edge_next[...]], axis=0)
        added = jnp.dot(pick, rows_all, preferred_element_type=F32)
        out_ref[...] = (hid_ref[...].astype(F32) + weight * added).astype(BF16)

        for d in used:
            d.wait_send()

    vmem = pl.BlockSpec(memory_space=pltpu.VMEM)
    hbm = pl.BlockSpec(memory_space=pl.ANY)
    blocks = (nx, 2, rows, feat)
    return pl.pallas_call(
        kernel,
        out_shape=jax.ShapeDtypeStruct((tok, feat), BF16),
        in_specs=[pl.BlockSpec(memory_space=pltpu.SMEM), vmem, vmem, vmem, vmem, hbm, hbm, hbm],
        out_specs=vmem,
        scratch_shapes=[
            pltpu.VMEM((feat, 2 * units), BF16),
            pltpu.VMEM((units, feat), BF16),
            pltpu.VMEM((ny, tok, 128), F32),
            pltpu.VMEM((8, 8, 128), F32),
            pltpu.VMEM((nz, 8, 128), F32),
            pltpu.VMEM((edge, feat), BF16),
            pltpu.VMEM((edge, feat), BF16),
            pltpu.VMEM((edge, feat), BF16),
            pltpu.VMEM((edge, feat), BF16),
            pltpu.VMEM((nz,) + blocks, BF16),
            pltpu.VMEM((nz, ny, own, 2 * units), BF16),
            pltpu.VMEM((nz, 2, own, units), BF16),
            pltpu.VMEM((nz, 2, 2, own, units), BF16),
            pltpu.VMEM((nz, ny, own, units), BF16),
            pltpu.VMEM((nz,) + blocks, BF16),
            pltpu.VMEM((nz, nx, rows, feat), BF16),
            pltpu.VMEM((nz, 2, rows, half), BF16),
            pltpu.VMEM((nz, 2, 2, rows, half), BF16),
            pltpu.VMEM((nz, rows, feat), BF16),
            pltpu.VMEM((nz - 1, rows, feat), BF16),
            pltpu.VMEM((edge, feat), BF16),
            pltpu.VMEM((edge, feat), BF16),
            pltpu.VMEM((edge, feat), BF16),
            pltpu.VMEM((edge, feat), BF16),
            pltpu.SemaphoreType.DMA((3,)),
            pltpu.SemaphoreType.DMA((N_SEM,)),
            pltpu.SemaphoreType.DMA((N_SEM,)),
        ],
        compiler_params=pltpu.CompilerParams(
            collective_id=0, has_side_effects=True, vmem_limit_bytes=56 * 1024 * 1024),
    )(counts, selected, router_weight.reshape(1, tok), norm_gain.reshape(1, feat), hidden,
      w_gate, w_up, w_down)


def solution(mesh):
    n_ctx, n_tp = mesh.shape["ctx"], mesh.shape["tp"]
    placed = (
        P("ctx", "tp"),
        P("ctx"),
        P("ctx", None),
        P("ctx"),
        P("tp"),
        P("tp", "ctx"),
        P("tp", "ctx"),
        P("ctx", "tp"),
    )

    def step(*args):
        return body(*args, n_ctx, n_tp)

    return jax.shard_map(
        step, mesh=mesh, in_specs=placed, out_specs=P("ctx", "tp"), check_vma=False
    )
```

time: 467 us -> 150 us (0.32)
  waiting for transfers between devices: 354 us -> 0 us
  Pallas kernels: 0 us -> 146 us
  matrix products: 42.7 us -> 0 us
  local copies, waits for them, and re-layouts: 30.7 us -> 1.77 us
  between operations: 14.5 us -> 0.66 us
  other arithmetic: 13.1 us -> 0 us
  blocking collectives: 10.8 us -> 0 us
    unnamed x5 -> x0, waiting for transfers between devices: 156 us -> none
    pallas_call x0 -> x1, Pallas kernels: none -> 146 us  [body(): pl.pallas_call(kernel, out_shape=jax.ShapeDtypeStruct((tok, feat), BF16),...]
    all_gather x2 -> x0, waiting for transfers between devices: 103 us -> none  [the longest x1 55.7 us: body(): piece = lax.all_gather(normed, 'ctx', axis=0, tiled=True)]
    reduce_scatter x1 -> x0, waiting for transfers between devices: 94.7 us -> none  [body(): lax.psum_scatter(jnp.dot(hidden, w_down, preferred_element_type=jnp.float...]
    dot_general x4 -> x0, matrix products: 42.7 us -> none  [the longest x1 15.3 us: body(): jnp.dot(hidden, w_down, preferred_element_type=jnp.float32)]
    another operation x1 -> x0, local copies, waits for them, and re-layouts: 23.2 us -> none  [body(): partial_units = jnp.stack([gate_part, up_part], axis=1)]
    psum x1 -> x0, blocking collectives: 10.8 us -> none  [body(): totals = lax.psum(squares, 'tp')]
    another operation x1 -> x0, other arithmetic: 6.17 us -> none  [body(): partial_units = jnp.stack([gate_part, up_part], axis=1)]
  transfers between devices with their start and end apart: 4 -> 0, of which waited for: 4 -> 0; matrix products, arithmetic and copies ran while one was open for 0% -> 0% of each run, Pallas kernels for 0% -> 0%
where the time goes in v1:
time: 150 us; the launch traced here: 148 us
  Pallas kernels  146 us (97%)
  local copies, waits for them, and re-layouts  1.77 us (1%)
    pallas_call x1, Pallas kernels, body(): pl.pallas_call(kernel, out_shape=jax.ShapeDtypeStruct((tok, feat), BF16),...  146 us

profile of v1, /device:TPU:0, one launch (start us, length us, event | category | flops | bytes accessed | tf_op | source)
XLA Modules:
  0.0 148.5 jit_solution(5648847954468799608)
XLA Ops:
  0.7 146.1 %shard_map.82 = bf16[96,2048]{1,0:T(8,128)(2,1)} custom-call(s32[1]{0:T(128)S(6)} %copy.10.counts_ref, s32[1,72]{1,0:T(1,128)} %sel_ref.1, f32[1,96]{1,0:T(1,128)} %bitcast.3, f32[1,2048]{1,0:T(1,128)} %bitcast.2, bf16[96,2048]{1,0:T(8,128)(2,1)} %hid_ref.1, bf16[2048,896]{1,0:T(8,128)(2,1)} %wg_hbm.1, bf16[2048,896]{1,0:T(8,128)(2,1)} %wu_hbm.1, ...), custom_call_target="tpu_custom_call" | custom-call | tf_op jit(solution)/shard_map/pallas_call | solution.py:344
  146.7 1.8 %copy.11 = bf16[96,2048]{1,0:T(8,128)(2,1)} copy(bf16[96,2048]{1,0:T(8,128)(2,1)} %shard_map.82) | data formatting | bytes 786432

commit v2 on v1

v2 whole, which is shorter than its diff:
```python
import jax
import jax.numpy as jnp
from jax import lax
from jax.experimental import pallas as pl
from jax.experimental.pallas import tpu as pltpu
from jax.sharding import PartitionSpec as P

MESH = pl.DeviceIdType.MESH
F32 = jnp.float32
BF16 = jnp.bfloat16
N_SEM = 224


def body(hidden, counts, selected, router_weight, norm_gain, w_gate, w_up, w_down, n_ctx, n_tp):
    tok, feat = hidden.shape
    most = selected.shape[1]
    units = w_gate.shape[1]
    width = feat * n_tp
    rows = most * 2 // 3
    edge = 16
    nx, nz, ny = 4, n_ctx // 8, n_tp
    fixed = 16

    def kernel(counts_ref, sel_ref, rw_ref, gain_ref, hid_ref, wg_hbm, wu_hbm, wd_hbm, out_ref,
               w_gu, w_dn, sq, cnt, ztot, to_prev, to_next, from_next, from_prev,
               x_buf, part, r1, r2, h_buf, y_buf, sib_buf, q1, t_buf, zr,
               edge_next, edge_prev, load_sem, send_sem, recv_sem):
        ctx = lax.axis_index("ctx")
        y = lax.axis_index("tp")
        z, q = ctx // 8, ctx % 8
        x, c = q // 2, q % 2

        def at(zz, xx, cc):
            return (zz * nx + xx) * 2 + cc

        xp, xm, x2 = (x + 1) % nx, (x + nx - 1) % nx, (x + 2) % nx
        zp, zm = (z + 1) % nz, (z + nz - 1) % nz
        yp, ym, y2 = (y + 1) % ny, (y + ny - 1) % ny, (y + 2) % ny
        sib = (at(z, x, 1 - c), y)
        d_xp, d_xm = (at(z, xp, c), y), (at(z, xm, c), y)
        d_zp, d_zm = (at(zp, x, c), y), (at(zm, x, c), y)
        d_yp, d_ym = (ctx, yp), (ctx, ym)
        d_next, d_prev = ((ctx + 1) % n_ctx, y), ((ctx + n_ctx - 1) % n_ctx, y)

        loads = []
        for i, (src, dst) in enumerate((
            (wg_hbm, w_gu.at[:, pl.ds(0, units)]),
            (wu_hbm, w_gu.at[:, pl.ds(units, units)]),
            (wd_hbm, w_dn),
        )):
            load = pltpu.make_async_copy(src, dst, load_sem.at[i])
            load.start()
            loads.append(load)

        used = []

        def copy(src, dst, dev):
            i = len(used)
            d = pltpu.make_async_remote_copy(
                src_ref=src, dst_ref=dst, send_sem=send_sem.at[i], recv_sem=recv_sem.at[i],
                device_id=dev, device_id_type=MESH)
            used.append(d)
            d.start()
            return d

        row_peers = [(at(z, (q + j) % 8 // 2, (q + j) % 8 % 2), y) for j in range(1, 8)]
        x_peers = [(at(z, (x + j) % nx, c), y) for j in range(1, nx)]
        z_peers = [(at((z + j) % nz, x, c), y) for j in range(1, nz)]
        y_peers = [(ctx, (y + j) % ny) for j in range(1, ny)]

        barrier = pltpu.get_barrier_semaphore()
        peers = row_peers + z_peers + y_peers + [d_next, d_prev]
        for dev in peers:
            pl.semaphore_signal(barrier, inc=1, device_id=dev, device_id_type=MESH)

        n_f = counts_ref[0].astype(F32)
        cnt[q] = jnp.full((8, 128), n_f, F32)
        hid = hid_ref[...].astype(F32)
        diagonal = (lax.broadcasted_iota(jnp.int32, (tok, 128), 0)
                    == lax.broadcasted_iota(jnp.int32, (tok, 128), 1))
        squares = jnp.sum(hid * hid, axis=-1, keepdims=True)
        sq[y] = jnp.broadcast_to(
            jnp.sum(jnp.where(diagonal, squares, 0.0), axis=0, keepdims=True), (8, 128))
        ids = lax.broadcasted_iota(jnp.int32, (tok, most), 0)
        rank = lax.broadcasted_iota(jnp.int32, (tok, most), 1).astype(F32)
        match = jnp.where((sel_ref[...] == ids) & (rank < n_f), 1.0, 0.0).astype(F32).astype(BF16)

        def chosen(count, offset, first, excess):
            slot = lax.broadcasted_iota(jnp.int32, (count, most), 0).astype(F32) + offset
            place = lax.broadcasted_iota(jnp.int32, (count, most), 1).astype(F32)
            here = (place < fixed) if first else (place >= fixed)
            shift = jnp.where((slot == place + excess) & here, 1.0, 0.0).astype(F32).astype(BF16)
            return lax.dot_general(
                shift, match, (((1,), (1,)), ((), ())), preferred_element_type=F32).astype(BF16)

        pl.semaphore_wait(barrier, len(peers))

        c_sq = [copy(sq.at[y], sq.at[y], dev) for dev in y_peers]
        c_row = [copy(cnt.at[q], cnt.at[q], dev) for dev in row_peers]
        for d in c_sq:
            d.wait_recv()
        sums = sq[0]
        for j in range(1, ny):
            sums = sums + sq[j]
        scale = lax.rsqrt(sums / width + 1e-05)[0:1]
        scale = jnp.sum(jnp.where(diagonal, scale, 0.0), axis=-1, keepdims=True)
        normed = (hid_ref[...].astype(F32) * scale * gain_ref[...]).astype(BF16)

        parts = ((0, fixed), (fixed, rows - fixed))
        rel = [x, xm, xp, x2]
        g_x, g_up, g_dn, g_sib = {}, {}, {}, {}

        def spread(p, i):
            xb, rs = rel[i], pl.ds(*parts[p])
            g_up[p, i] = copy(x_buf.at[0, xb, c, rs], x_buf.at[3, xb, c, rs], d_zp)
            g_dn[p, i] = copy(x_buf.at[0, xb, c, rs], x_buf.at[1, xb, c, rs], d_zm)
            g_sib[0, p, i] = copy(x_buf.at[0, xb, c, rs], x_buf.at[0, xb, c, rs], sib)

        def share(k, p):
            rs = pl.ds(*parts[p])
            g_sib[k, p] = copy(x_buf.at[k, :, c, rs], x_buf.at[k, :, c, rs], sib)

        def offer(p):
            rs = pl.ds(*parts[p])
            g_x[p] = [copy(x_buf.at[0, x, c, rs], x_buf.at[0, x, c, rs], dev) for dev in x_peers]
            spread(p, 0)

        def take(p, n):
            i, j = ((1, 0), (2, 2), (3, 1))[n]
            g_x[p][j].wait_recv()
            spread(p, i)

        x_buf[0, x, c, pl.ds(0, fixed)] = jnp.dot(
            chosen(fixed, 0, True, 0.0), normed, preferred_element_type=F32).astype(BF16)
        offer(0)

        for d in c_row:
            d.wait_recv()
        before = jnp.zeros((8, 128), F32)
        total = jnp.zeros((8, 128), F32)
        for j in range(8):
            before = before + cnt[j] * jnp.where(j < q, 1.0, 0.0).astype(F32)
            total = total + cnt[j]
        ztot[z] = total
        c_z = [copy(ztot.at[z], ztot.at[z], dev) for dev in z_peers]

        take(0, 0)
        take(0, 1)
        take(0, 2)
        loads[0].wait()
        loads[1].wait()
        for d in c_z:
            d.wait_recv()
        for j in range(nz):
            before = before + ztot[j] * jnp.where(j < z, 1.0, 0.0).astype(F32)
        excess = (before - (ctx * rows).astype(F32))[0:1, 0:1]
        to_prev[...] = jnp.dot(
            chosen(edge, 0, False, excess), normed, preferred_element_type=F32).astype(BF16)
        c_prev = copy(to_prev, from_next, d_prev)
        to_next[...] = jnp.dot(
            chosen(edge, rows, False, excess), normed, preferred_element_type=F32).astype(BF16)
        c_next = copy(to_next, from_prev, d_next)
        x_buf[0, x, c, pl.ds(fixed, rows - fixed)] = jnp.dot(
            chosen(rows - fixed, fixed, False, excess), normed, preferred_element_type=F32
        ).astype(BF16)

        def settle_rows():
            for d, got, r0 in ((c_next, from_prev, fixed), (c_prev, from_next, rows - edge)):
                d.wait_recv()
                x_buf[0, x, c, pl.ds(r0, edge)] = (
                    x_buf[0, x, c, pl.ds(r0, edge)].astype(F32) + got[...].astype(F32)
                ).astype(BF16)
            offer(1)

        subs = ((0, 0, 16), (1, 0, 16), (3, 0, 16), (2, 0, 16), (0, 16, 32), (2, 16, 32), (3, 16, 32), (1, 16, 32))
        waited = set()
        gate, up = pl.ds(0, units), pl.ds(units, units)
        steps = (2 * units) // 256
        y_first, y_second, y_gather, y_pass = {}, {}, {}, {}

        def gate_up(s):
            k, r0, nr = subs[s]
            rs = pl.ds(r0, nr)
            for p, (first, count) in enumerate(parts):
                if first < r0 + nr and r0 < first + count and (k, p) not in waited:
                    waited.add((k, p))
                    for d in [g_sib[0, p, i] for i in range(4)] if k == 0 else [g_sib[k, p]]:
                        d.wait_recv()

            def tile(j, carry):
                cols = pl.ds(pl.multiple_of(j * 256, 256), 256)
                res = jnp.dot(x_buf[k, :, :, rs].reshape(nx * 2 * nr, feat), w_gu[:, cols],
                              preferred_element_type=F32)
                part[k, :, :, rs, cols] = res.astype(BF16).reshape(ny, 2, nr, 256)
                return carry

            lax.fori_loop(0, steps, tile, 0)
            y_first[s] = (copy(part.at[k, y2, :, rs, gate], r1.at[k, 0, :, rs], d_yp),
                          copy(part.at[k, y2, :, rs, up], r1.at[k, 1, :, rs], d_ym))
            y_second[s] = [copy(part.at[k, yp, :, rs, up], r2.at[k, 0, 1, :, rs], d_yp),
                           copy(part.at[k, ym, :, rs, gate], r2.at[k, 1, 0, :, rs], d_ym)]

        def combine(s):
            k, r0, nr = subs[s]
            rs = pl.ds(r0, nr)
            y_first[s][0].wait_recv()
            part[k, yp, :, rs, gate] = (
                part[k, yp, :, rs, gate].astype(F32) + r1[k, 0, :, rs].astype(F32)).astype(BF16)
            y_second[s].append(copy(part.at[k, yp, :, rs, gate], r2.at[k, 0, 0, :, rs], d_yp))
            y_first[s][1].wait_recv()
            part[k, ym, :, rs, up] = (
                part[k, ym, :, rs, up].astype(F32) + r1[k, 1, :, rs].astype(F32)).astype(BF16)
            y_second[s].append(copy(part.at[k, ym, :, rs, up], r2.at[k, 1, 1, :, rs], d_ym))

        def activate(s):
            k, r0, nr = subs[s]
            rs = pl.ds(r0, nr)
            for d in y_second[s]:
                d.wait_recv()
            g = (part[k, y, :, rs, gate].astype(F32) + r2[k, 0, 0, :, rs].astype(F32)
                 + r2[k, 1, 0, :, rs].astype(F32))
            u = (part[k, y, :, rs, up].astype(F32) + r2[k, 0, 1, :, rs].astype(F32)
                 + r2[k, 1, 1, :, rs].astype(F32))
            h_buf[k, y, :, rs] = (g / (1.0 + jnp.exp(-g)) * u).astype(BF16)
            mine = h_buf.at[k, y, :, rs]
            y_gather[s] = (copy(mine, mine, d_yp), copy(mine, mine, d_ym))

        def pass_on(s):
            k, r0, nr = subs[s]
            rs = pl.ds(r0, nr)
            y_gather[s][0].wait_recv()
            left = h_buf.at[k, ym, 0, rs]
            f_p = copy(left, left, d_yp)
            y_gather[s][1].wait_recv()
            right = h_buf.at[k, yp, 1, rs]
            f_m = copy(right, right, d_ym)
            y_pass[s] = (f_p, f_m)

        s_core, s_x, s_z = {}, {}, {}

        def down(s):
            k, r0, nr = subs[s]
            rs = pl.ds(r0, nr)
            for d in y_pass[s]:
                d.wait_recv()

            def tile(j, carry):
                cols = pl.ds(pl.multiple_of(j * 256, 256), 256)
                res = jnp.dot(h_buf[k, :, :, rs].reshape(nx * 2 * nr, units), w_dn[:, cols],
                              preferred_element_type=F32)
                y_buf[k, :, :, rs, cols] = res.astype(BF16).reshape(nx, 2, nr, 256)
                return carry

            lax.fori_loop(0, feat // 256, tile, 0)
            s_core[s] = copy(y_buf.at[k, :, 1 - c, rs], sib_buf.at[k, :, rs], sib)

        def fold(s):
            k, r0, nr = subs[s]
            rs = pl.ds(r0, nr)
            s_core[s].wait_recv()
            s_x[s] = []
            for j in (2, 1, 3, 0):
                xb = (x + j) % nx
                y_buf[k, xb, c, rs] = (
                    y_buf[k, xb, c, rs].astype(F32) + sib_buf[k, xb, rs].astype(F32)).astype(BF16)
                if j:
                    s_x[s].append(copy(y_buf.at[k, xb, c, rs], q1.at[k, nx - j - 1, rs],
                                       x_peers[j - 1]))

        def settle(s):
            k, r0, nr = subs[s]
            rs = pl.ds(r0, nr)
            for d in s_x[s]:
                d.wait_recv()
            t_buf[k, rs] = (
                y_buf[k, x, c, rs].astype(F32) + q1[k, 0, rs].astype(F32)
                + q1[k, 1, rs].astype(F32) + q1[k, 2, rs].astype(F32)).astype(BF16)
            if k:
                s_z[s] = copy(t_buf.at[k, rs], zr.at[(nz - k) % nz - 1, rs], z_peers[k - 1])

        def z_take(p, i):
            xb, rs = rel[i], pl.ds(*parts[p])
            g_up[p, i].wait_recv()
            g_dn[p, i].wait_recv()
            k, dev = ((3, d_zp), (1, d_zm))[i % 2]
            forward[p].append(copy(x_buf.at[k, xb, c, rs], x_buf.at[2, xb, c, rs], dev))
            if i == 3:
                share(1, p)
                share(3, p)

        def z_last(p):
            for d in forward[p]:
                d.wait_recv()
            share(2, p)

        forward = ([], [])
        z_take(0, 0)
        gate_up(0)
        settle_rows()
        z_take(0, 1)
        z_take(0, 2)
        z_take(0, 3)
        combine(0)
        gate_up(2)
        activate(0)
        take(1, 0)
        gate_up(1)
        take(1, 1)
        z_last(0)
        combine(2)
        take(1, 2)
        gate_up(3)
        gate_up(4)
        combine(1)
        activate(2)
        z_take(1, 0)
        z_take(1, 1)
        z_take(1, 2)
        z_take(1, 3)
        combine(3)
        gate_up(7)
        pass_on(0)
        activate(3)
        gate_up(6)
        pass_on(3)
        activate(1)
        combine(4)
        pass_on(1)
        combine(7)
        loads[2].wait()
        down(0)
        pass_on(2)
        down(3)
        z_last(1)
        fold(0)
        activate(4)
        down(1)
        activate(7)
        down(2)
        combine(6)
        pass_on(4)
        fold(3)
        gate_up(5)
        fold(2)
        fold(1)
        pass_on(7)
        down(4)
        fold(4)
        activate(6)
        combine(5)
        down(7)
        settle(3)
        pass_on(6)
        fold(7)
        activate(5)
        down(6)
        pass_on(5)
        settle(2)
        settle(4)
        fold(6)
        down(5)
        fold(5)
        settle(7)
        settle(1)
        settle(0)
        settle(6)
        settle(5)

        for s in s_z:
            s_z[s].wait_recv()
        ffn = t_buf[0].astype(F32)
        for k in range(1, nz):
            ffn = ffn + zr[k - 1].astype(F32)
        t_buf[0] = ffn.astype(BF16)
        e_prev = copy(t_buf.at[0, pl.ds(fixed, edge)], edge_next, d_prev)
        e_next = copy(t_buf.at[0, pl.ds(rows - edge, edge)], edge_prev, d_next)
        span = rows + 2 * edge
        slot = lax.broadcasted_iota(jnp.int32, (most, span), 1).astype(F32)
        place = lax.broadcasted_iota(jnp.int32, (most, span), 0).astype(F32)
        aim = jnp.where(place < fixed, place, place + excess + fixed)
        shift = jnp.where(slot == aim, 1.0, 0.0).astype(F32).astype(BF16)
        pick = jnp.dot(match, shift, preferred_element_type=F32).astype(BF16)
        line = lax.broadcasted_iota(jnp.int32, (tok, tok), 0)
        col = lax.broadcasted_iota(jnp.int32, (tok, tok), 1)
        weight = jnp.sum(jnp.where(line == col, rw_ref[...], 0.0), axis=-1, keepdims=True)
        e_prev.wait_recv()
        e_next.wait_recv()
        rows_all = jnp.concatenate(
            [t_buf[0, pl.ds(0, fixed)], edge_prev[...], t_buf[0, pl.ds(fixed, rows - fixed)],
             edge_next[...]], axis=0)
        added = jnp.dot(pick, rows_all, preferred_element_type=F32)
        out_ref[...] = (hid_ref[...].astype(F32) + weight * added).astype(BF16)

        for d in used:
            d.wait_send()

    vmem = pl.BlockSpec(memory_space=pltpu.VMEM)
    hbm = pl.BlockSpec(memory_space=pl.ANY)
    blocks = (nx, 2, rows, feat)
    return pl.pallas_call(
        kernel,
        out_shape=jax.ShapeDtypeStruct((tok, feat), BF16),
        in_specs=[pl.BlockSpec(memory_space=pltpu.SMEM), vmem, vmem, vmem, vmem, hbm, hbm, hbm],
        out_specs=vmem,
        scratch_shapes=[
            pltpu.VMEM((feat, 2 * units), BF16),
            pltpu.VMEM((units, feat), BF16),
            pltpu.VMEM((ny, 8, 128), F32),
            pltpu.VMEM((8, 8, 128), F32),
            pltpu.VMEM((nz, 8, 128), F32),
            pltpu.VMEM((edge, feat), BF16),
            pltpu.VMEM((edge, feat), BF16),
            pltpu.VMEM((edge, feat), BF16),
            pltpu.VMEM((edge, feat), BF16),
            pltpu.VMEM((nz,) + blocks, BF16),
            pltpu.VMEM((nz, ny, 2, rows, 2 * units), BF16),
            pltpu.VMEM((nz, 2, 2, rows, units), BF16),
            pltpu.VMEM((nz, 2, 2, 2, rows, units), BF16),
            pltpu.VMEM((nz, ny, 2, rows, units), BF16),
            pltpu.VMEM((nz,) + blocks, BF16),
            pltpu.VMEM((nz, nx, rows, feat), BF16),
            pltpu.VMEM((nz, nx - 1, rows, feat), BF16),
            pltpu.VMEM((nz, rows, feat), BF16),
            pltpu.VMEM((nz - 1, rows, feat), BF16),
            pltpu.VMEM((edge, feat), BF16),
            pltpu.VMEM((edge, feat), BF16),
            pltpu.SemaphoreType.DMA((3,)),
            pltpu.SemaphoreType.DMA((N_SEM,)),
            pltpu.SemaphoreType.DMA((N_SEM,)),
        ],
        compiler_params=pltpu.CompilerParams(
            collective_id=0, has_side_effects=True, vmem_limit_bytes=56 * 1024 * 1024),
    )(counts, selected, router_weight.reshape(1, tok), norm_gain.reshape(1, feat), hidden,
      w_gate, w_up, w_down)


def solution(mesh):
    n_ctx, n_tp = mesh.shape["ctx"], mesh.shape["tp"]
    placed = (
        P("ctx", "tp"),
        P("ctx"),
        P("ctx", None),
        P("ctx"),
        P("tp"),
        P("tp", "ctx"),
        P("tp", "ctx"),
        P("ctx", "tp"),
    )

    def step(*args):
        return body(*args, n_ctx, n_tp)

    return jax.shard_map(
        step, mesh=mesh, in_specs=placed, out_specs=P("ctx", "tp"), check_vma=False
    )
```

time: 150 us -> 125 us (0.83)
  Pallas kernels: 146 us -> 122 us
    pallas_call x1, Pallas kernels: 146 us -> 122 us  [body(): pl.pallas_call(kernel, out_shape=jax.ShapeDtypeStruct((tok, feat), BF16),...]
where the time goes in v2:
time: 125 us; the launch traced here: 124 us
  Pallas kernels  122 us (98%)
  local copies, waits for them, and re-layouts  1.77 us (1%)
    pallas_call x1, Pallas kernels, body(): pl.pallas_call(kernel, out_shape=jax.ShapeDtypeStruct((tok, feat), BF16),...  122 us

profile of v2, /device:TPU:0, one launch (start us, length us, event | category | flops | bytes accessed | tf_op | source)
XLA Modules:
  0.0 124.4 jit_solution(2143681748627709036)
XLA Ops:
  0.7 122.0 %shard_map.82 = bf16[96,2048]{1,0:T(8,128)(2,1)} custom-call(s32[1]{0:T(128)S(6)} %copy.10.counts_ref, s32[1,72]{1,0:T(1,128)} %sel_ref.1, f32[1,96]{1,0:T(1,128)} %bitcast.3, f32[1,2048]{1,0:T(1,128)} %bitcast.2, bf16[96,2048]{1,0:T(8,128)(2,1)} %hid_ref.1, bf16[2048,896]{1,0:T(8,128)(2,1)} %wg_hbm.1, bf16[2048,896]{1,0:T(8,128)(2,1)} %wu_hbm.1, ...), custom_call_target="tpu_custom_call" | custom-call | tf_op jit(solution)/shard_map/pallas_call | solution.py:400
  122.6 1.8 %copy.11 = bf16[96,2048]{1,0:T(8,128)(2,1)} copy(bf16[96,2048]{1,0:T(8,128)(2,1)} %shard_map.82) | data formatting | bytes 786432

commit v3 on v2

--- a/solution.py
+++ b/solution.py
@@ -173,6 +173,7 @@
             offer(1)
 
         subs = ((0, 0, 16), (1, 0, 16), (3, 0, 16), (2, 0, 16), (0, 16, 32), (2, 16, 32), (3, 16, 32), (1, 16, 32))
+        direct = (0,)
         waited = set()
         gate, up = pl.ds(0, units), pl.ds(units, units)
         steps = (2 * units) // 256
@@ -187,14 +188,20 @@
                     for d in [g_sib[0, p, i] for i in range(4)] if k == 0 else [g_sib[k, p]]:
                         d.wait_recv()
 
-            def tile(j, carry):
-                cols = pl.ds(pl.multiple_of(j * 256, 256), 256)
+            for j in range(steps):
+                cols = pl.ds(j * 256, 256)
                 res = jnp.dot(x_buf[k, :, :, rs].reshape(nx * 2 * nr, feat), w_gu[:, cols],
                               preferred_element_type=F32)
                 part[k, :, :, rs, cols] = res.astype(BF16).reshape(ny, 2, nr, 256)
-                return carry
-
-            lax.fori_loop(0, steps, tile, 0)
+            if s in direct:
+                y_second[s] = [
+                    copy(part.at[k, owner, :, rs, cols], place.at[:, rs], dev)
+                    for owner, dev, places in (
+                        (y2, (ctx, y2), (r1.at[k, 0], r1.at[k, 1])),
+                        (yp, d_yp, (r2.at[k, 0, 0], r2.at[k, 0, 1])),
+                        (ym, d_ym, (r2.at[k, 1, 0], r2.at[k, 1, 1])))
+                    for cols, place in zip((gate, up), places)]
+                return
             y_first[s] = (copy(part.at[k, y2, :, rs, gate], r1.at[k, 0, :, rs], d_yp),
                           copy(part.at[k, y2, :, rs, up], r1.at[k, 1, :, rs], d_ym))
             y_second[s] = [copy(part.at[k, yp, :, rs, up], r2.at[k, 0, 1, :, rs], d_yp),
@@ -221,9 +228,14 @@
                  + r2[k, 1, 0, :, rs].astype(F32))
             u = (part[k, y, :, rs, up].astype(F32) + r2[k, 0, 1, :, rs].astype(F32)
                  + r2[k, 1, 1, :, rs].astype(F32))
+            if s in direct:
+                g = g + r1[k, 0, :, rs].astype(F32)
+                u = u + r1[k, 1, :, rs].astype(F32)
             h_buf[k, y, :, rs] = (g / (1.0 + jnp.exp(-g)) * u).astype(BF16)
             mine = h_buf.at[k, y, :, rs]
             y_gather[s] = (copy(mine, mine, d_yp), copy(mine, mine, d_ym))
+            if s in direct:
+                y_pass[s] = y_gather[s] + (copy(mine, mine, (ctx, y2)),)
 
         def pass_on(s):
             k, r0, nr = subs[s]
@@ -244,14 +256,11 @@
             for d in y_pass[s]:
                 d.wait_recv()
 
-            def tile(j, carry):
-                cols = pl.ds(pl.multiple_of(j * 256, 256), 256)
+            for j in range(feat // 256):
+                cols = pl.ds(j * 256, 256)
                 res = jnp.dot(h_buf[k, :, :, rs].reshape(nx * 2 * nr, units), w_dn[:, cols],
                               preferred_element_type=F32)
                 y_buf[k, :, :, rs, cols] = res.astype(BF16).reshape(nx, 2, nr, 256)
-                return carry
-
-            lax.fori_loop(0, feat // 256, tile, 0)
             s_core[s] = copy(y_buf.at[k, :, 1 - c, rs], sib_buf.at[k, :, rs], sib)
 
         def fold(s):
@@ -293,6 +302,24 @@
                 d.wait_recv()
             share(2, p)
 
+        arrived, edges = set(), []
+
+        def finish_rows(r0, nr):
+            rs = pl.ds(r0, nr)
+            for s, (k, first, count) in enumerate(subs):
+                if k and first < r0 + nr and r0 < first + count and s not in arrived:
+                    arrived.add(s)
+                    s_z[s].wait_recv()
+            ffn = t_buf[0, rs].astype(F32)
+            for k in range(1, nz):
+                ffn = ffn + zr[k - 1, rs].astype(F32)
+            t_buf[0, rs] = ffn.astype(BF16)
+
+        def send_edges():
+            finish_rows(fixed, rows - fixed)
+            edges.append(copy(t_buf.at[0, pl.ds(fixed, edge)], edge_next, d_prev))
+            edges.append(copy(t_buf.at[0, pl.ds(rows - edge, edge)], edge_prev, d_next))
+
         forward = ([], [])
         z_take(0, 0)
         gate_up(0)
@@ -300,80 +327,72 @@
         z_take(0, 1)
         z_take(0, 2)
         z_take(0, 3)
-        combine(0)
+        gate_up(1)
+        take(1, 0)
+        take(1, 1)
         gate_up(2)
-        activate(0)
-        take(1, 0)
-        gate_up(1)
-        take(1, 1)
         z_last(0)
-        combine(2)
         take(1, 2)
         gate_up(3)
+        z_take(1, 0)
+        combine(1)
         gate_up(4)
-        combine(1)
-        activate(2)
-        z_take(1, 0)
+        activate(0)
         z_take(1, 1)
         z_take(1, 2)
+        combine(3)
         z_take(1, 3)
-        combine(3)
-        gate_up(7)
-        pass_on(0)
-        activate(3)
+        activate(1)
         gate_up(6)
-        pass_on(3)
-        activate(1)
-        combine(4)
-        pass_on(1)
-        combine(7)
         loads[2].wait()
         down(0)
+        gate_up(7)
+        pass_on(1)
+        combine(6)
+        z_last(1)
+        combine(7)
+        combine(2)
+        fold(0)
+        down(1)
+        activate(6)
+        gate_up(5)
+        activate(7)
+        pass_on(6)
+        combine(5)
+        pass_on(7)
+        combine(4)
+        fold(1)
+        down(6)
+        activate(2)
+        fold(6)
+        activate(5)
+        down(7)
+        settle(1)
         pass_on(2)
+        activate(4)
+        fold(7)
+        pass_on(5)
+        down(2)
+        fold(2)
+        down(5)
+        pass_on(4)
+        fold(5)
+        settle(6)
+        activate(3)
+        down(4)
+        pass_on(3)
+        fold(4)
+        settle(2)
+        settle(7)
+        settle(0)
         down(3)
-        z_last(1)
-        fold(0)
-        activate(4)
-        down(1)
-        activate(7)
-        down(2)
-        combine(6)
-        pass_on(4)
+        settle(5)
         fold(3)
-        gate_up(5)
-        fold(2)
-        fold(1)
-        pass_on(7)
-        down(4)
-        fold(4)
-        activate(6)
-        combine(5)
-        down(7)
+        settle(4)
+        send_edges()
         settle(3)
-        pass_on(6)
-        fold(7)
-        activate(5)
-        down(6)
-        pass_on(5)
-        settle(2)
-        settle(4)
-        fold(6)
-        down(5)
-        fold(5)
-        settle(7)
-        settle(1)
-        settle(0)
-        settle(6)
-        settle(5)
-
-        for s in s_z:
-            s_z[s].wait_recv()
-        ffn = t_buf[0].astype(F32)
-        for k in range(1, nz):
-            ffn = ffn + zr[k - 1].astype(F32)
-        t_buf[0] = ffn.astype(BF16)
-        e_prev = copy(t_buf.at[0, pl.ds(fixed, edge)], edge_next, d_prev)
-        e_next = copy(t_buf.at[0, pl.ds(rows - edge, edge)], edge_prev, d_next)
+
+        finish_rows(0, fixed)
         span = rows + 2 * edge
         slot = lax.broadcasted_iota(jnp.int32, (most, span), 1).astype(F32)
         place = lax.broadcasted_iota(jnp.int32, (most, span), 0).astype(F32)
@@ -383,8 +402,8 @@
         line = lax.broadcasted_iota(jnp.int32, (tok, tok), 0)
         col = lax.broadcasted_iota(jnp.int32, (tok, tok), 1)
         weight = jnp.sum(jnp.where(line == col, rw_ref[...], 0.0), axis=-1, keepdims=True)
-        e_prev.wait_recv()
-        e_next.wait_recv()
+        for d in edges:
+            d.wait_recv()
         rows_all = jnp.concatenate(
             [t_buf[0, pl.ds(0, fixed)], edge_prev[...], t_buf[0, pl.ds(fixed, rows - fixed)],
              edge_next[...]], axis=0)

time: 125 us -> 120 us (0.960)
  Pallas kernels: 122 us -> 117 us
    pallas_call x1, Pallas kernels: 122 us -> 117 us  [body(): pl.pallas_call(kernel, out_shape=jax.ShapeDtypeStruct((tok, feat), BF16),...]
where the time goes in v3:
time: 120 us; the launch traced here: 119 us
  Pallas kernels  117 us (98%)
  local copies, waits for them, and re-layouts  1.77 us (1%)
    pallas_call x1, Pallas kernels, body(): pl.pallas_call(kernel, out_shape=jax.ShapeDtypeStruct((tok, feat), BF16),...  117 us

profile of v3, /device:TPU:0, one launch (start us, length us, event | category | flops | bytes accessed | tf_op | source)
XLA Modules:
  0.0 119.2 jit_solution(9424589135607189088)
XLA Ops:
  0.7 116.8 %shard_map.82 = bf16[96,2048]{1,0:T(8,128)(2,1)} custom-call(s32[1]{0:T(128)S(6)} %copy.10.counts_ref, s32[1,72]{1,0:T(1,128)} %sel_ref.1, f32[1,96]{1,0:T(1,128)} %bitcast.3, f32[1,2048]{1,0:T(1,128)} %bitcast.2, bf16[96,2048]{1,0:T(8,128)(2,1)} %hid_ref.1, bf16[2048,896]{1,0:T(8,128)(2,1)} %wg_hbm.1, bf16[2048,896]{1,0:T(8,128)(2,1)} %wu_hbm.1, ...), custom_call_target="tpu_custom_call" | custom-call | tf_op jit(solution)/shard_map/pallas_call | solution.py:419
  117.4 1.8 %copy.11 = bf16[96,2048]{1,0:T(8,128)(2,1)} copy(bf16[96,2048]{1,0:T(8,128)(2,1)} %shard_map.82) | data formatting | bytes 786432

commit v4 on v3

--- a/solution.py
+++ b/solution.py
@@ -21,8 +21,8 @@
     nx, nz, ny = 4, n_ctx // 8, n_tp
     fixed = 16
 
-    def kernel(counts_ref, sel_ref, rw_ref, gain_ref, hid_ref, wg_hbm, wu_hbm, wd_hbm, out_ref,
-               w_gu, w_dn, sq, cnt, ztot, to_prev, to_next, from_next, from_prev,
+    def kernel(cnt_hbm, sel_hbm, gain_hbm, hid_hbm, wg_hbm, wu_hbm, wd_hbm, out_ref,
+               cnt_ref, sel_ref, gain_ref, hid_ref, w_gu, w_dn, sq, cnt, ztot, to_prev, to_next, from_next, from_prev,
                x_buf, part, r1, r2, h_buf, y_buf, sib_buf, q1, t_buf, zr,
                edge_next, edge_prev, load_sem, send_sem, recv_sem):
         ctx = lax.axis_index("ctx")
@@ -44,6 +44,10 @@
 
         loads = []
         for i, (src, dst) in enumerate((
+            (hid_hbm, hid_ref),
+            (cnt_hbm, cnt_ref),
+            (sel_hbm, sel_ref),
+            (gain_hbm, gain_ref),
             (wg_hbm, w_gu.at[:, pl.ds(0, units)]),
             (wu_hbm, w_gu.at[:, pl.ds(units, units)]),
             (wd_hbm, w_dn),
@@ -73,8 +77,10 @@
         for dev in peers:
             pl.semaphore_signal(barrier, inc=1, device_id=dev, device_id_type=MESH)
 
-        n_f = counts_ref[0].astype(F32)
-        cnt[q] = jnp.full((8, 128), n_f, F32)
+        for load in loads[:4]:
+            load.wait()
+        n_f = cnt_ref[...].astype(F32)
+        cnt[q] = jnp.broadcast_to(n_f, (8, 128))
         hid = hid_ref[...].astype(F32)
         diagonal = (lax.broadcasted_iota(jnp.int32, (tok, 128), 0)
                     == lax.broadcasted_iota(jnp.int32, (tok, 128), 1))
@@ -93,6 +99,9 @@
             return lax.dot_general(
                 shift, match, (((1,), (1,)), ((), ())), preferred_element_type=F32).astype(BF16)
 
+        pick_fixed = chosen(fixed, 0, True, 0.0)
+        raw = jnp.dot(pick_fixed, hid_ref[...], preferred_element_type=F32)
+
         pl.semaphore_wait(barrier, len(peers))
 
         c_sq = [copy(sq.at[y], sq.at[y], dev) for dev in y_peers]
@@ -102,9 +111,10 @@
         sums = sq[0]
         for j in range(1, ny):
             sums = sums + sq[j]
-        scale = lax.rsqrt(sums / width + 1e-05)[0:1]
-        scale = jnp.sum(jnp.where(diagonal, scale, 0.0), axis=-1, keepdims=True)
-        normed = (hid_ref[...].astype(F32) * scale * gain_ref[...]).astype(BF16)
+        scale_row = lax.rsqrt(sums / width + 1e-05)[0:1]
+        scale_fixed = jnp.sum(
+            pick_fixed.astype(F32) * scale_row[:, 0:tok], axis=-1, keepdims=True)
+        x_buf[0, x, c, pl.ds(0, fixed)] = (raw * scale_fixed * gain_ref[...]).astype(BF16)
 
         parts = ((0, fixed), (fixed, rows - fixed))
         rel = [x, xm, xp, x2]
@@ -130,9 +140,9 @@
             g_x[p][j].wait_recv()
             spread(p, i)
 
-        x_buf[0, x, c, pl.ds(0, fixed)] = jnp.dot(
-            chosen(fixed, 0, True, 0.0), normed, preferred_element_type=F32).astype(BF16)
         offer(0)
+        scale = jnp.sum(jnp.where(diagonal, scale_row, 0.0), axis=-1, keepdims=True)
+        normed = (hid_ref[...].astype(F32) * scale * gain_ref[...]).astype(BF16)
 
         for d in c_row:
             d.wait_recv()
@@ -147,8 +157,8 @@
         take(0, 0)
         take(0, 1)
         take(0, 2)
-        loads[0].wait()
-        loads[1].wait()
+        loads[4].wait()
+        loads[5].wait()
         for d in c_z:
             d.wait_recv()
         for j in range(nz):
@@ -188,24 +198,34 @@
                     for d in [g_sib[0, p, i] for i in range(4)] if k == 0 else [g_sib[k, p]]:
                         d.wait_recv()
 
-            for j in range(steps):
+            def column(j):
                 cols = pl.ds(j * 256, 256)
                 res = jnp.dot(x_buf[k, :, :, rs].reshape(nx * 2 * nr, feat), w_gu[:, cols],
                               preferred_element_type=F32)
                 part[k, :, :, rs, cols] = res.astype(BF16).reshape(ny, 2, nr, 256)
+
+            ready = -(-units // 256)
+            sent = {}
+            for kind, cols, tiles in ((0, gate, range(ready)), (1, up, range(ready, steps))):
+                for j in tiles:
+                    column(j)
+                first, second = ((y2, d_yp), (y2, d_ym))[kind], ((ym, d_ym), (yp, d_yp))[kind]
+                if s in direct:
+                    sent[kind] = [copy(part.at[k, owner, :, rs, cols], place.at[:, rs], dev)
+                                  for owner, dev, place in (
+                                      (y2, (ctx, y2), r1.at[k, kind]),
+                                      (yp, d_yp, r2.at[k, 0, kind]),
+                                      (ym, d_ym, r2.at[k, 1, kind]))]
+                else:
+                    sent[kind] = (
+                        copy(part.at[k, first[0], :, rs, cols], r1.at[k, kind, :, rs], first[1]),
+                        copy(part.at[k, second[0], :, rs, cols], r2.at[k, 1 - kind, kind, :, rs],
+                             second[1]))
             if s in direct:
-                y_second[s] = [
-                    copy(part.at[k, owner, :, rs, cols], place.at[:, rs], dev)
-                    for owner, dev, places in (
-                        (y2, (ctx, y2), (r1.at[k, 0], r1.at[k, 1])),
-                        (yp, d_yp, (r2.at[k, 0, 0], r2.at[k, 0, 1])),
-                        (ym, d_ym, (r2.at[k, 1, 0], r2.at[k, 1, 1])))
-                    for cols, place in zip((gate, up), places)]
-                return
-            y_first[s] = (copy(part.at[k, y2, :, rs, gate], r1.at[k, 0, :, rs], d_yp),
-                          copy(part.at[k, y2, :, rs, up], r1.at[k, 1, :, rs], d_ym))
-            y_second[s] = [copy(part.at[k, yp, :, rs, up], r2.at[k, 0, 1, :, rs], d_yp),
-                           copy(part.at[k, ym, :, rs, gate], r2.at[k, 1, 0, :, rs], d_ym)]
+                y_second[s] = sent[0] + sent[1]
+            else:
+                y_first[s] = (sent[0][0], sent[1][0])
+                y_second[s] = [sent[0][1], sent[1][1]]
 
         def combine(s):
             k, r0, nr = subs[s]
@@ -321,94 +341,92 @@
             edges.append(copy(t_buf.at[0, pl.ds(rows - edge, edge)], edge_prev, d_next))
 
         forward = ([], [])
+        settle_rows()
         z_take(0, 0)
         gate_up(0)
-        settle_rows()
         z_take(0, 1)
         z_take(0, 2)
         z_take(0, 3)
         gate_up(1)
         take(1, 0)
         take(1, 1)
-        gate_up(2)
+        take(1, 2)
+        activate(0)
+        gate_up(4)
         z_last(0)
-        take(1, 2)
+        loads[6].wait()
+        down(0)
         gate_up(3)
         z_take(1, 0)
-        combine(1)
-        gate_up(4)
-        activate(0)
+        combine(4)
         z_take(1, 1)
         z_take(1, 2)
-        combine(3)
         z_take(1, 3)
-        activate(1)
+        gate_up(7)
         gate_up(6)
-        loads[2].wait()
-        down(0)
-        gate_up(7)
-        pass_on(1)
+        activate(4)
         combine(6)
         z_last(1)
         combine(7)
-        combine(2)
-        fold(0)
-        down(1)
+        pass_on(4)
         activate(6)
         gate_up(5)
-        activate(7)
+        down(4)
         pass_on(6)
         combine(5)
+        fold(4)
+        activate(7)
+        fold(0)
+        activate(5)
+        down(6)
         pass_on(7)
-        combine(4)
+        gate_up(2)
+        fold(6)
+        combine(3)
+        pass_on(5)
+        down(7)
+        combine(1)
+        fold(7)
+        activate(3)
+        combine(2)
+        down(5)
+        activate(1)
+        pass_on(3)
+        settle(0)
+        fold(5)
+        activate(2)
+        down(3)
+        pass_on(1)
+        pass_on(2)
+        settle(6)
+        fold(3)
+        settle(7)
+        down(1)
         fold(1)
-        down(6)
-        activate(2)
-        fold(6)
-        activate(5)
-        down(7)
+        settle(5)
+        down(2)
+        settle(4)
+        fold(2)
+        settle(3)
+        send_edges()
         settle(1)
-        pass_on(2)
-        activate(4)
-        fold(7)
-        pass_on(5)
-        down(2)
-        fold(2)
-        down(5)
-        pass_on(4)
-        fold(5)
-        settle(6)
-        activate(3)
-        down(4)
-        pass_on(3)
-        fold(4)
         settle(2)
-        settle(7)
-        settle(0)
-        down(3)
-        settle(5)
-        fold(3)
-        settle(4)
-        send_edges()
-        settle(3)
-
-        finish_rows(0, fixed)
+
         span = rows + 2 * edge
         slot = lax.broadcasted_iota(jnp.int32, (most, span), 1).astype(F32)
         place = lax.broadcasted_iota(jnp.int32, (most, span), 0).astype(F32)
         aim = jnp.where(place < fixed, place, place + excess + fixed)
         shift = jnp.where(slot == aim, 1.0, 0.0).astype(F32).astype(BF16)
         pick = jnp.dot(match, shift, preferred_element_type=F32).astype(BF16)
-        line = lax.broadcasted_iota(jnp.int32, (tok, tok), 0)
-        col = lax.broadcasted_iota(jnp.int32, (tok, tok), 1)
-        weight = jnp.sum(jnp.where(line == col, rw_ref[...], 0.0), axis=-1, keepdims=True)
         for d in edges:
             d.wait_recv()
-        rows_all = jnp.concatenate(
-            [t_buf[0, pl.ds(0, fixed)], edge_prev[...], t_buf[0, pl.ds(fixed, rows - fixed)],
-             edge_next[...]], axis=0)
-        added = jnp.dot(pick, rows_all, preferred_element_type=F32)
-        out_ref[...] = (hid_ref[...].astype(F32) + weight * added).astype(BF16)
+        others = jnp.concatenate(
+            [edge_prev[...], t_buf[0, pl.ds(fixed, rows - fixed)], edge_next[...]], axis=0)
+        base = jnp.dot(pick[:, fixed:], others, preferred_element_type=F32)
+        finish_rows(0, fixed)
+        added = base + jnp.dot(
+            pick[:, 0:fixed], t_buf[0, pl.ds(0, fixed)], preferred_element_type=F32)
+        out_ref[...] = added.astype(BF16)
 
         for d in used:
             d.wait_send()
@@ -416,12 +434,16 @@
     vmem = pl.BlockSpec(memory_space=pltpu.VMEM)
     hbm = pl.BlockSpec(memory_space=pl.ANY)
     blocks = (nx, 2, rows, feat)
-    return pl.pallas_call(
+    added = pl.pallas_call(
         kernel,
         out_shape=jax.ShapeDtypeStruct((tok, feat), BF16),
-        in_specs=[pl.BlockSpec(memory_space=pltpu.SMEM), vmem, vmem, vmem, vmem, hbm, hbm, hbm],
+        in_specs=[hbm] * 7,
         out_specs=vmem,
         scratch_shapes=[
+            pltpu.VMEM((1, 1), jnp.int32),
+            pltpu.VMEM((1, most), jnp.int32),
+            pltpu.VMEM((1, feat), F32),
+            pltpu.VMEM((tok, feat), BF16),
             pltpu.VMEM((feat, 2 * units), BF16),
             pltpu.VMEM((units, feat), BF16),
             pltpu.VMEM((ny, 8, 128), F32),
@@ -443,14 +465,14 @@
             pltpu.VMEM((nz - 1, rows, feat), BF16),
             pltpu.VMEM((edge, feat), BF16),
             pltpu.VMEM((edge, feat), BF16),
-            pltpu.SemaphoreType.DMA((3,)),
+            pltpu.SemaphoreType.DMA((7,)),
             pltpu.SemaphoreType.DMA((N_SEM,)),
             pltpu.SemaphoreType.DMA((N_SEM,)),
         ],
         compiler_params=pltpu.CompilerParams(
             collective_id=0, has_side_effects=True, vmem_limit_bytes=56 * 1024 * 1024),
-    )(counts, selected, router_weight.reshape(1, tok), norm_gain.reshape(1, feat), hidden,
-      w_gate, w_up, w_down)
+    )(counts.reshape(1, 1), selected, norm_gain.reshape(1, feat), hidden, w_gate, w_up, w_down)
+    return (hidden.astype(F32) + router_weight[:, None] * added.astype(F32)).astype(BF16)
 
 
 def solution(mesh):

time: 120 us -> 115 us (0.958)
  Pallas kernels: 117 us -> 112 us
  other arithmetic: 0 us -> 1.93 us
  local copies, waits for them, and re-layouts: 1.77 us -> 0.01 us
    pallas_call x1, Pallas kernels: 117 us -> 112 us  [body(): pl.pallas_call(kernel, out_shape=jax.ShapeDtypeStruct((tok, feat), BF16),...]
    convert_element_type x0 -> x1, other arithmetic: none -> 1.93 us  [body(): (hidden.astype(F32) + router_weight[:, None] * added.astype(F32)).astype(...]
    unnamed x1 -> x4, local copies, waits for them, and re-layouts: 1.77 us -> 0.01 us
where the time goes in v4:
time: 115 us
  Pallas kernels  112 us (97%)
  other arithmetic  1.93 us (2%)
    pallas_call x1, Pallas kernels, body(): pl.pallas_call(kernel, out_shape=jax.ShapeDtypeStruct((tok, feat), BF16),...  112 us

profile of v4, /device:TPU:0, one launch (start us, length us, event | category | flops | bytes accessed | tf_op | source)
XLA Modules:
  0.0 114.6 jit_solution(17681118271040360661)
XLA Ops:
  0.7 0.0 copy-start
  0.7 0.0 copy-start.1
  0.7 111.9 %shard_map.82 = bf16[96,2048]{1,0:T(8,128)(2,1)} custom-call(s32[1,1]{1,0:T(1,128)} %bitcast.2.cnt_hbm, s32[1,72]{1,0:T(1,128)} %sel_hbm.1, f32[1,2048]{1,0:T(1,128)} %bitcast.3, bf16[96,2048]{1,0:T(8,128)(2,1)} %hid_hbm.1, bf16[2048,896]{1,0:T(8,128)(2,1)} %wg_hbm.1, bf16[2048,896]{1,0:T(8,128)(2,1)} %wu_hbm.1, bf16[896,2048]{1,0:T(8,128)(2,1)} %wd_hbm.1), custom_call_target="tpu_custom_call" | custom-call | tf_op jit(solution)/shard_map/pallas_call | solution.py:437
  112.6 0.0 copy-done
  112.6 0.0 copy-done.1
  112.6 1.9 %add_convert_fusion = bf16[96,2048]{1,0:T(8,128)(2,1)} fusion(bf16[96,2048]{1,0:T(8,128)(2,1)} %shard_map.82, bf16[96,2048]{1,0:T(8,128)(2,1)S(1)} %copy-done, f32[96]{0:T(128)S(1)} %copy-done.1), kind=kLoop, calls=%fused_computation | loop fusion | flops 983040 | bytes 1180032 | tf_op jit(solution)/shard_map/convert_element_type | solution.py:475
Async XLA Ops:
  0.7 112.0 %copy-start = (bf16[96,2048]{1,0:T(8,128)(2,1)S(1)}, bf16[96,2048]{1,0:T(8,128)(2,1)}, u32[]{:S(2)}) copy-start(bf16[96,2048]{1,0:T(8,128)(2,1)} %hid_hbm.1) | copy-start | bytes 1179652
  0.7 112.0 %copy-start.1 = (f32[96]{0:T(128)S(1)}, f32[96]{0:T(128)}, u32[]{:S(2)}) copy-start(f32[96]{0:T(128)} %param.11) | copy-start | bytes 1156

commit v5 on v4

--- a/solution.py
+++ b/solution.py
@@ -41,6 +41,27 @@
         d_zp, d_zm = (at(zp, x, c), y), (at(zm, x, c), y)
         d_yp, d_ym = (ctx, yp), (ctx, ym)
         d_next, d_prev = ((ctx + 1) % n_ctx, y), ((ctx + n_ctx - 1) % n_ctx, y)
+
+        used = []
+
+        def copy(src, dst, dev):
+            i = len(used)
+            d = pltpu.make_async_remote_copy(
+                src_ref=src, dst_ref=dst, send_sem=send_sem.at[i], recv_sem=recv_sem.at[i],
+                device_id=dev, device_id_type=MESH)
+            used.append(d)
+            d.start()
+            return d
+
+        row_peers = [(at(z, (q + j) % 8 // 2, (q + j) % 8 % 2), y) for j in range(1, 8)]
+        x_peers = [(at(z, (x + j) % nx, c), y) for j in range(1, nx)]
+        z_peers = [(at((z + j) % nz, x, c), y) for j in range(1, nz)]
+        y_peers = [(ctx, (y + j) % ny) for j in range(1, ny)]
+
+        barrier = pltpu.get_barrier_semaphore()
+        peers = row_peers + z_peers + y_peers + [d_next, d_prev]
+        for dev in peers:
+            pl.semaphore_signal(barrier, inc=1, device_id=dev, device_id_type=MESH)
 
         loads = []
         for i, (src, dst) in enumerate((
@@ -56,27 +77,6 @@
             load.start()
             loads.append(load)
 
-        used = []
-
-        def copy(src, dst, dev):
-            i = len(used)
-            d = pltpu.make_async_remote_copy(
-                src_ref=src, dst_ref=dst, send_sem=send_sem.at[i], recv_sem=recv_sem.at[i],
-                device_id=dev, device_id_type=MESH)
-            used.append(d)
-            d.start()
-            return d
-
-        row_peers = [(at(z, (q + j) % 8 // 2, (q + j) % 8 % 2), y) for j in range(1, 8)]
-        x_peers = [(at(z, (x + j) % nx, c), y) for j in range(1, nx)]
-        z_peers = [(at((z + j) % nz, x, c), y) for j in range(1, nz)]
-        y_peers = [(ctx, (y + j) % ny) for j in range(1, ny)]
-
-        barrier = pltpu.get_barrier_semaphore()
-        peers = row_peers + z_peers + y_peers + [d_next, d_prev]
-        for dev in peers:
-            pl.semaphore_signal(barrier, inc=1, device_id=dev, device_id_type=MESH)
-
         for load in loads[:4]:
             load.wait()
         n_f = cnt_ref[...].astype(F32)
@@ -87,6 +87,10 @@
         squares = jnp.sum(hid * hid, axis=-1, keepdims=True)
         sq[y] = jnp.broadcast_to(
             jnp.sum(jnp.where(diagonal, squares, 0.0), axis=0, keepdims=True), (8, 128))
+        pl.semaphore_wait(barrier, len(peers))
+
+        c_sq = [copy(sq.at[y], sq.at[y], dev) for dev in y_peers]
+        c_row = [copy(cnt.at[q], cnt.at[q], dev) for dev in row_peers]
         ids = lax.broadcasted_iota(jnp.int32, (tok, most), 0)
         rank = lax.broadcasted_iota(jnp.int32, (tok, most), 1).astype(F32)
         match = jnp.where((sel_ref[...] == ids) & (rank < n_f), 1.0, 0.0).astype(F32).astype(BF16)
@@ -101,11 +105,6 @@
 
         pick_fixed = chosen(fixed, 0, True, 0.0)
         raw = jnp.dot(pick_fixed, hid_ref[...], preferred_element_type=F32)
-
-        pl.semaphore_wait(barrier, len(peers))
-
-        c_sq = [copy(sq.at[y], sq.at[y], dev) for dev in y_peers]
-        c_row = [copy(cnt.at[q], cnt.at[q], dev) for dev in row_peers]
         for d in c_sq:
             d.wait_recv()
         sums = sq[0]
@@ -132,7 +131,9 @@
 
         def offer(p):
             rs = pl.ds(*parts[p])
-            g_x[p] = [copy(x_buf.at[0, x, c, rs], x_buf.at[0, x, c, rs], dev) for dev in x_peers]
+            far, near_p, near_m = (
+                copy(x_buf.at[0, x, c, rs], x_buf.at[0, x, c, rs], x_peers[j]) for j in (1, 0, 2))
+            g_x[p] = [near_p, far, near_m]
             spread(p, 0)
 
         def take(p, n):
@@ -184,7 +185,13 @@
 
         subs = ((0, 0, 16), (1, 0, 16), (3, 0, 16), (2, 0, 16), (0, 16, 32), (2, 16, 32), (3, 16, 32), (1, 16, 32))
         direct = (0,)
+        fine = ()
         waited = set()
+
+        def spans(s):
+            n = 2 if s in fine else 1
+            return [pl.ds(i * (feat // n), feat // n) for i in range(n)]
+
         gate, up = pl.ds(0, units), pl.ds(units, units)
         steps = (2 * units) // 256
         y_first, y_second, y_gather, y_pass = {}, {}, {}, {}
@@ -276,36 +283,46 @@
             for d in y_pass[s]:
                 d.wait_recv()
 
-            for j in range(feat // 256):
-                cols = pl.ds(j * 256, 256)
-                res = jnp.dot(h_buf[k, :, :, rs].reshape(nx * 2 * nr, units), w_dn[:, cols],
-                              preferred_element_type=F32)
-                y_buf[k, :, :, rs, cols] = res.astype(BF16).reshape(nx, 2, nr, 256)
-            s_core[s] = copy(y_buf.at[k, :, 1 - c, rs], sib_buf.at[k, :, rs], sib)
+            s_core[s] = []
+            for cut in spans(s):
+                for j in range(cut.start // 256, (cut.start + cut.size) // 256):
+                    cols = pl.ds(j * 256, 256)
+                    res = jnp.dot(h_buf[k, :, :, rs].reshape(nx * 2 * nr, units), w_dn[:, cols],
+                                  preferred_element_type=F32)
+                    y_buf[k, :, :, rs, cols] = res.astype(BF16).reshape(nx, 2, nr, 256)
+                s_core[s].append(
+                    copy(y_buf.at[k, :, 1 - c, rs, cut], sib_buf.at[k, :, rs, cut], sib))
 
         def fold(s):
             k, r0, nr = subs[s]
             rs = pl.ds(r0, nr)
-            s_core[s].wait_recv()
             s_x[s] = []
-            for j in (2, 1, 3, 0):
-                xb = (x + j) % nx
-                y_buf[k, xb, c, rs] = (
-                    y_buf[k, xb, c, rs].astype(F32) + sib_buf[k, xb, rs].astype(F32)).astype(BF16)
-                if j:
-                    s_x[s].append(copy(y_buf.at[k, xb, c, rs], q1.at[k, nx - j - 1, rs],
-                                       x_peers[j - 1]))
+            for cut, arriving in zip(spans(s), s_core[s]):
+                arriving.wait_recv()
+                sent = []
+                for j in (2, 1, 3, 0):
+                    xb = (x + j) % nx
+                    y_buf[k, xb, c, rs, cut] = (
+                        y_buf[k, xb, c, rs, cut].astype(F32)
+                        + sib_buf[k, xb, rs, cut].astype(F32)).astype(BF16)
+                    if j:
+                        sent.append(copy(y_buf.at[k, xb, c, rs, cut],
+                                         q1.at[k, nx - j - 1, rs, cut], x_peers[j - 1]))
+                s_x[s].append(sent)
 
         def settle(s):
             k, r0, nr = subs[s]
             rs = pl.ds(r0, nr)
-            for d in s_x[s]:
-                d.wait_recv()
-            t_buf[k, rs] = (
-                y_buf[k, x, c, rs].astype(F32) + q1[k, 0, rs].astype(F32)
-                + q1[k, 1, rs].astype(F32) + q1[k, 2, rs].astype(F32)).astype(BF16)
-            if k:
-                s_z[s] = copy(t_buf.at[k, rs], zr.at[(nz - k) % nz - 1, rs], z_peers[k - 1])
+            s_z[s] = []
+            for cut, sent in zip(spans(s), s_x[s]):
+                for d in sent:
+                    d.wait_recv()
+                t_buf[k, rs, cut] = (
+                    y_buf[k, x, c, rs, cut].astype(F32) + q1[k, 0, rs, cut].astype(F32)
+                    + q1[k, 1, rs, cut].astype(F32) + q1[k, 2, rs, cut].astype(F32)).astype(BF16)
+                if k:
+                    s_z[s].append(copy(t_buf.at[k, rs, cut], zr.at[(nz - k) % nz - 1, rs, cut],
+                                       z_peers[k - 1]))
 
         def z_take(p, i):
             xb, rs = rel[i], pl.ds(*parts[p])
@@ -329,7 +346,8 @@
             for s, (k, first, count) in enumerate(subs):
                 if k and first < r0 + nr and r0 < first + count and s not in arrived:
                     arrived.add(s)
-                    s_z[s].wait_recv()
+                    for d in s_z[s]:
+                        d.wait_recv()
             ffn = t_buf[0, rs].astype(F32)
             for k in range(1, nz):
                 ffn = ffn + zr[k - 1, rs].astype(F32)

time: 115 us -> 114 us (level)
  no operation moved by 1% of the time
where the time goes in v5:
time: 114 us
  Pallas kernels  112 us (98%)
  other arithmetic  1.93 us (2%)
    pallas_call x1, Pallas kernels, body(): pl.pallas_call(kernel, out_shape=jax.ShapeDtypeStruct((tok, feat), BF16),...  112 us

profile of v5, /device:TPU:0, one launch (start us, length us, event | category | flops | bytes accessed | tf_op | source)
XLA Modules:
  0.0 114.2 jit_solution(13156101239525696376)
XLA Ops:
  0.7 0.0 copy-start
  0.7 0.0 copy-start.1
  0.7 111.6 %shard_map.82 = bf16[96,2048]{1,0:T(8,128)(2,1)} custom-call(s32[1,1]{1,0:T(1,128)} %bitcast.2.cnt_hbm, s32[1,72]{1,0:T(1,128)} %sel_hbm.1, f32[1,2048]{1,0:T(1,128)} %bitcast.3, bf16[96,2048]{1,0:T(8,128)(2,1)} %hid_hbm.1, bf16[2048,896]{1,0:T(8,128)(2,1)} %wg_hbm.1, bf16[2048,896]{1,0:T(8,128)(2,1)} %wu_hbm.1, bf16[896,2048]{1,0:T(8,128)(2,1)} %wd_hbm.1), custom_call_target="tpu_custom_call" | custom-call | tf_op jit(solution)/shard_map/pallas_call | solution.py:455
  112.3 0.0 copy-done
  112.3 0.0 copy-done.1
  112.3 1.9 %add_convert_fusion = bf16[96,2048]{1,0:T(8,128)(2,1)} fusion(bf16[96,2048]{1,0:T(8,128)(2,1)} %shard_map.82, bf16[96,2048]{1,0:T(8,128)(2,1)S(1)} %copy-done, f32[96]{0:T(128)S(1)} %copy-done.1), kind=kLoop, calls=%fused_computation | loop fusion | flops 983040 | bytes 1180032 | tf_op jit(solution)/shard_map/convert_element_type | solution.py:493
Async XLA Ops:
  0.7 111.6 %copy-start = (bf16[96,2048]{1,0:T(8,128)(2,1)S(1)}, bf16[96,2048]{1,0:T(8,128)(2,1)}, u32[]{:S(2)}) copy-start(bf16[96,2048]{1,0:T(8,128)(2,1)} %hid_hbm.1) | copy-start | bytes 1179652
  0.7 111.6 %copy-start.1 = (f32[96]{0:T(128)S(1)}, f32[96]{0:T(128)}, u32[]{:S(2)}) copy-start(f32[96]{0:T(128)} %param.11) | copy-start | bytes 1156
